TPU v7x, 256 devices: a whole 4x4x8 slice. The times are simulated.
256 devices in a mesh: dp: 32 (over y, x, core), tensor: 8 (over z).
Axes of the slice: x: 4, y: 4, z: 8, core: 2. Of those that a mesh axis runs over, the one named last changes fastest.
Arguments:
- rank_query: bfloat16 [256, 32, 5120], P('dp', None, 'tensor'), may hold values from -4.5 to 4.5
- rank_key: bfloat16 [256, 32, 5120], P('dp', None, 'tensor'), may hold values from -4.5 to 4.5
- rank_value: bfloat16 [256, 32, 5120], P('dp', None, 'tensor'), may hold values from -6 to 6
- rank_resid: bfloat16 [256, 32, 5120], P(('dp', 'tensor')), may hold values from -4 to 4
- out_weight: bfloat16 [5120, 5120], P('tensor', 'dp'), may hold values from -0.25 to 0.25
- rank_gain: bfloat16 [5120], replicated, may hold values from 0.099609375 to 1.8984375
- score_weight: bfloat16 [5120], replicated, may hold values from -0.078125 to 0.078125
- pair_index: int32 [256, 3], P(('dp', 'tensor')), may hold values from 0 to 31, as said below
- cand_rank: int32 [1024, 8], P('dp'), may hold values from 0 to 7, each once within a row
- cand_len: int32 [1024, 8], P('dp'), may hold values from 1 to 8, 39 in all within a row
- blend_owner: int32 [32, 32], P('dp'), may hold values from 0 to 31, each once within a row
- blend_rows: bfloat16 [1024, 8, 8, 4096], P('dp', None, None, 'tensor'), may hold values from -6 to 6
- blend_gain: bfloat16 [4096], replicated, may hold values from 0.099609375 to 1.8984375
- blend_weight: bfloat16 [4096, 3, 2048], P('dp', None, 'tensor'), may hold values from -0.09375 to 0.09375
Outputs:
- rank_hidden: bfloat16 [256, 32, 5120], P(('dp', 'tensor'))
- cand_score: float32 [1024, 8], P('dp')
- blended_qkv: bfloat16 [1024, 24, 3, 2048], P('dp', None, None, 'tensor')
Inputs may be any that keep to these rules, and one draw needn't show every extreme that they name: `pair_index`: column 0 is a prompt of the pair's own group of 32 prompts (pair p belongs to group p // 8); columns 1 and 2 are two different candidates of that prompt. `cand_rank`: each row gives every rank once. `blend_owner`: each row names every group once.
All inputs are finite; a program needn't handle non-finite values.
Results may differ from a plain program's by a relative error of at most 0.024.
Values may be sent and summed in bfloat16 or wider, within the bound.
No kernel may reach another device: no remote copies, remote signals or barrier semaphores. Data moves between devices by JAX's collectives and lax.ppermute only.
A program may use at most 128 MiB of HBM per device.

v0:
```python
import math
import jax
import jax.numpy as jnp
from jax import lax
from jax.sharding import PartitionSpec as P

HR = 40
HDR = 128


def pair_attention(queries, keys_in, values_in, head_count):
    pair_count, length, row_width = queries.shape
    head_size = row_width // head_count
    query_heads = queries.reshape(pair_count, length, head_count, head_size)
    key_heads = keys_in.reshape(pair_count, length, head_count, head_size)
    value_heads = values_in.reshape(pair_count, length, head_count, head_size)
    scores = jnp.einsum(
        "pihd,pjhd->phij", query_heads, key_heads, preferred_element_type=jnp.float32
    ) * (1.0 / math.sqrt(HDR))
    highest = jnp.max(scores, axis=-1, keepdims=True)
    weights = jnp.exp(scores - highest)
    soft_weights = (weights / jnp.sum(weights, axis=-1, keepdims=True)).astype(jnp.bfloat16)
    context = jnp.einsum(
        "phij,pjhd->pihd", soft_weights, value_heads, preferred_element_type=jnp.float32
    )
    return context.astype(jnp.bfloat16).reshape(pair_count * length, row_width)


def encode(rows_in, blend_gain, blend_weight):
    whole_rows = lax.all_gather(rows_in, "tensor", axis=3, tiled=True)
    prompts, pick_count, length, features = whole_rows.shape
    flat_rows = whole_rows.reshape(prompts * pick_count * length, features)
    as_float = flat_rows.astype(jnp.float32)
    scale_rows = lax.rsqrt(jnp.mean(as_float * as_float, axis=-1, keepdims=True) + 1e-06)
    blend_normed = (as_float * scale_rows * blend_gain.astype(jnp.float32)).astype(jnp.bfloat16)
    columns = blend_weight.shape[1] * blend_weight.shape[2]
    portion = lax.all_gather(blend_weight, "dp", axis=0, tiled=True)
    projected = jnp.dot(
        blend_normed, portion.reshape(portion.shape[0], columns), preferred_element_type=jnp.float32
    )
    return projected.astype(jnp.bfloat16).reshape(
        prompts, pick_count * length, blend_weight.shape[1], blend_weight.shape[2]
    )


def body(
    rank_query,
    rank_key,
    rank_value,
    rank_resid,
    out_weight,
    rank_gain,
    score_weight,
    pair_index,
    cand_rank,
    cand_len,
    blend_owner,
    blend_rows,
    blend_gain,
    blend_weight,
):
    tensor_count = lax.axis_size("tensor")
    local_heads = HR // tensor_count
    length = rank_query.shape[1]
    context = pair_attention(rank_query, rank_key, rank_value, local_heads)
    own_pairs = rank_resid.shape[0]
    own_rows = own_pairs * length
    term_rows = jnp.dot(
        context,
        lax.all_gather(out_weight, "dp", axis=1, tiled=True),
        preferred_element_type=jnp.float32,
    )
    summed = lax.psum(term_rows.astype(jnp.bfloat16), "tensor").astype(jnp.float32)
    part_sum = lax.dynamic_slice_in_dim(summed, lax.axis_index("tensor") * own_rows, own_rows, 0)
    mixed_rows = rank_resid.reshape(own_rows, -1).astype(jnp.float32) + part_sum
    mean_square = jnp.mean(mixed_rows * mixed_rows, axis=-1, keepdims=True)
    normed = mixed_rows * lax.rsqrt(mean_square + 1e-05) * rank_gain.astype(jnp.float32)
    rank_hidden = normed.astype(jnp.bfloat16).reshape(rank_resid.shape)
    leading = normed.reshape(own_pairs, length, -1)[:, 0, :]
    pair_logit = jnp.sum(leading * score_weight.astype(jnp.float32), axis=-1)
    prompt_count = cand_rank.shape[0]
    cand_count = cand_rank.shape[1]
    slot_ids = jnp.arange(prompt_count * cand_count, dtype=jnp.int32)
    base_slot = pair_index[:, 0] * cand_count
    upward = jnp.where(
        (base_slot + pair_index[:, 1])[:, None] == slot_ids[None, :], pair_logit[:, None], 0.0
    )
    downward = jnp.where(
        (base_slot + pair_index[:, 2])[:, None] == slot_ids[None, :], pair_logit[:, None], 0.0
    )
    vote_sums = jnp.sum(upward - downward, axis=0).reshape(prompt_count, cand_count)
    cand_score = lax.psum(vote_sums, "tensor")
    places = jnp.arange(3, dtype=jnp.int32)
    matched = cand_rank[:, None, :] == places[None, :, None]
    labels = jnp.arange(cand_count, dtype=jnp.int32)
    chosen = jnp.sum(jnp.where(matched, labels[None, None, :], 0), axis=-1)
    chosen_len = jnp.sum(jnp.where(matched, cand_len[:, None, :], 0), axis=-1)
    prompt_ids = jnp.arange(prompt_count, dtype=jnp.int32)
    picked = blend_rows[prompt_ids[:, None], chosen]
    positions = jnp.arange(blend_rows.shape[2], dtype=jnp.int32)
    live_rows = positions[None, None, :] < chosen_len[:, :, None]
    picked = jnp.where(live_rows[..., None], picked, jnp.zeros((), jnp.bfloat16))
    owners = blend_owner[0]
    sender = jnp.sum(
        jnp.where(owners[None, :] == prompt_ids[:, None], prompt_ids[None, :], 0), axis=1
    )
    outgoing = picked[sender]
    arrived = lax.all_to_all(outgoing, "dp", split_axis=0, concat_axis=0, tiled=True)
    blended_qkv = encode(arrived, blend_gain, blend_weight)
    return (rank_hidden, cand_score, blended_qkv)


def solution(mesh):
    placed = (
        P("dp", None, "tensor"),
        P("dp", None, "tensor"),
        P("dp", None, "tensor"),
        P(("dp", "tensor"), None, None),
        P("tensor", "dp"),
        P(),
        P(),
        P(("dp", "tensor"), None),
        P("dp", None),
        P("dp", None),
        P("dp", None),
        P("dp", None, None, "tensor"),
        P(),
        P("dp", None, "tensor"),
    )
    return jax.shard_map(
        body,
        mesh=mesh,
        in_specs=placed,
        out_specs=(P(("dp", "tensor"), None, None), P("dp", None), P("dp", None, None, "tensor")),
        check_vma=False,
    )
```

profile of v0, /device:TPU:2, one launch (start us, length us, event | category | flops | bytes accessed | tf_op | source)
XLA Modules:
  0.0 343.9 jit_solution(1360914309973684097)
XLA Ops:
  7.2 0.0 copy-start
  7.2 0.0 copy-start.3
  7.2 0.0 copy-start.2
  7.2 0.0 all-gather.6.cloned.1.call-start
  7.2 0.9 select_reduce_fusion.2
  8.1 0.1 copy.60
  8.2 0.1 reshape.142
  8.3 0.1 copy.59
  8.4 0.1 iota_compare_fusion
  8.5 0.8 select_reduce_fusion
  9.3 0.6 pad_clamp_fusion
  9.9 0.0 copy-done
  9.9 2.0 gather_fusion
  11.9 1.3 broadcast_select_fusion
  13.3 0.0 copy-start.5
  13.3 0.0 copy-start.6
  13.3 1.7 gather_fusion.1
  15.0 21.0 %all_to_all.5 = bf16[32,3,8,512]{3,2,1,0:T(8,128)(2,1)} all-to-all(bf16[32,3,8,512]{3,2,1,0:T(8,128)(2,1)} %gather_fusion.1), channel_id=1, replica_groups=mesh['dp'=32,'tensor'=8] {'dp'}, dimensions={0} | all-to-all | bytes 1572864 | tf_op jit(solution)/shard_map/all_to_all | solution.py:108
  36.0 0.0 all-gather.6.cloned.1.call-update
  36.1 0.0 all-gather.4.cloned.1.call-start
  36.1 0.7 all-gather.4.cloned.1.call-update
  36.8 0.0 all-gather.8.cloned.1.call-start
  36.9 1.7 copy.63
  38.6 0.0 all-gather.8.cloned.1.call-update
  38.6 0.0 all-reduce.2.cloned.1.call-start
  38.7 0.0 copy-done.3
  38.7 0.0 copy-done.2
  38.7 1.0 fusion.32
  39.7 0.3 convolution_multiply_fusion
  40.0 1.3 fusion.6
  41.3 0.2 copy.58
  41.5 0.0 copy-done.5
  41.5 0.0 copy-done.6
  41.5 0.6 fusion.31
  44.0 0.7 convert_element_type.58
  44.7 66.2 %all-gather.6.cloned.1.call-done = bf16[32,3,8,4096]{3,2,1,0:T(8,128)(2,1)} async-done(((bf16[32,3,8,512]{3,2,1,0:T(8,128)(2,1)}), bf16[32,3,8,4096]{3,2,1,0:T(8,128)(2,1)}) %all-gather.6.cloned.1.call-update) | async-done | bytes 6291472 | tf_op jit(solution)/shard_map/all_gather | solution.py:30
  110.9 4.1 %fusion.1 = f32[32,3,8]{2,1,0:T(4,128)S(1)} fusion(bf16[32,3,8,4096]{3,2,1,0:T(8,128)(2,1)} %all-gather.6.cloned.1.call-done), kind=kLoop, calls=%fused_computation.5 | loop fusion | flops 9436416 | bytes 6294528 | tf_op jit(solution)/shard_map/reduce_sum | solution.py:34
  115.0 0.1 copy.61
  115.1 0.1 copy.62
  115.2 50.6 %all-gather.4.cloned.1.call-done = bf16[640,5120]{0,1:T(8,128)(2,1)} async-done(((bf16[640,160]{0,1:T(8,128)(2,1)}), bf16[640,5120]{0,1:T(8,128)(2,1)}) %all-gather.4.cloned.1.call-update) | async-done | bytes 6553616 | tf_op jit(solution)/shard_map/all_gather | solution.py:70
  165.7 6.6 %convolution_convert_fusion = bf16[256,5120]{1,0:T(8,128)(2,1)} fusion(bf16[640,5120]{0,1:T(8,128)(2,1)} %all-gather.4.cloned.1.call-done, bf16[32,8,5,128]{3,2,1,0:T(8,128)(2,1)S(1)} %bitcast.74), kind=kOutput, calls=%fused_computation.8 | convolution fusion | flops 1679032320 | bytes 9502720 | tf_op jit(solution)/shard_map/dot_general | solution.py:68
  172.3 0.0 all-reduce.2.cloned.1.call-update
  172.4 8.2 %fusion.3 = bf16[32,3,8,4096]{3,2,1,0:T(8,128)(2,1)} fusion(bf16[32,3,8,4096]{3,2,1,0:T(8,128)(2,1)} %all-gather.6.cloned.1.call-done, f32[4096]{0:T(1024)S(1)} %convert_element_type.58, f32[32,3,8]{2,1,0:T(4,128)S(1)} %copy.62), kind=kLoop, calls=%fused_computation.7 | loop fusion | flops 12582912 | bytes 12602368 | tf_op jit(solution)/shard_map/convert_element_type | solution.py:35
  180.5 47.1 %all-gather.8.cloned.1.call-done = bf16[4096,3,256]{0,2,1:T(8,128)(2,1)} async-done(((bf16[128,3,256]{0,2,1:T(8,128)(2,1)}), bf16[4096,3,256]{0,2,1:T(8,128)(2,1)}) %all-gather.8.cloned.1.call-update) | async-done | bytes 6291472 | tf_op jit(solution)/shard_map/all_gather | solution.py:37
  227.7 0.0 copy-start.1
  227.7 9.9 %convolution_convert_fusion.1 = bf16[768,768]{1,0:T(8,128)(2,1)} fusion(bf16[768,4096]{1,0:T(8,128)(2,1)} %bitcast.72, bf16[4096,768]{0,1:T(8,128)(2,1)} %bitcast.76), kind=kOutput, calls=%fused_computation.9 | convolution fusion | flops 4832428032 | bytes 13762560 | tf_op jit(solution)/shard_map/dot_general | solution.py:38
  237.6 0.0 copy-start.4
  237.6 3.7 %reshape.140 = bf16[32,24,3,256]{3,2,1,0:T(4,128)(2,1)} reshape(bf16[768,768]{1,0:T(8,128)(2,1)} %convolution_convert_fusion.1) | data formatting | bytes 2359296 | tf_op jit(solution)/shard_map/reshape | solution.py:41
  241.3 2.6 copy.64
  243.9 72.1 %all-reduce.2.cloned.1.call-done = bf16[256,5120]{1,0:T(8,128)(2,1)} async-done(((bf16[256,5120]{1,0:T(8,128)(2,1)}), bf16[256,5120]{1,0:T(8,128)(2,1)}) %all-reduce.2.cloned.1.call-update) | async-done | bytes 2621456 | tf_op jit(solution)/shard_map/psum | solution.py:73
  316.0 0.0 copy-done.1
  316.0 1.2 multiply_reduce_fusion
  317.2 1.8 fusion.7
  319.1 0.0 copy-done.4
  319.1 0.6 multiply_reduce_fusion.1
  319.7 0.6 select_subtract_fusion
  320.2 17.1 %psum.15 = f32[32,8]{0,1:T(8,128)} all-reduce(f32[32,8]{0,1:T(8,128)S(1)} %select_subtract_fusion), channel_id=1, replica_groups=mesh['dp'=32,'tensor'=8] {'tensor'}, use_global_device_ids=true, to_apply=%region_5.6 | all-reduce | flops 256 | bytes 2048 | tf_op jit(solution)/shard_map/psum | solution.py:92
  (6 shorter events, 0.1 us)
Async XLA Ops:
  7.2 2.7 copy-start
  7.2 31.5 %copy-start.3 = (bf16[8,32,640]{2,1,0:T(8,128)(2,1)S(1)}, bf16[8,32,640]{2,1,0:T(8,128)(2,1)}, u32[]{:S(2)}) copy-start(bf16[8,32,640]{2,1,0:T(8,128)(2,1)} %param.14) | copy-start | bytes 983044
  7.2 31.5 %copy-start.2 = (bf16[8,32,640]{2,1,0:T(8,128)(2,1)S(1)}, bf16[8,32,640]{2,1,0:T(8,128)(2,1)}, u32[]{:S(2)}) copy-start(bf16[8,32,640]{2,1,0:T(8,128)(2,1)} %param.15) | copy-start | bytes 983044
  7.2 103.7 %all-gather.6.cloned.1.call-start = ((), (), s32[]{:S(2)}) async-start(), calls=%async_computation.3 | async-start | bytes 7077888 | tf_op jit(solution)/shard_map/all_gather | solution.py:30
  13.3 28.3 %copy-start.5 = (bf16[5120]{0:T(1024)(128)(2,1)S(1)}, bf16[5120]{0:T(1024)(128)(2,1)}, u32[]{:S(2)}) copy-start(bf16[5120]{0:T(1024)(128)(2,1)} %param.19) | copy-start | bytes 30724
  13.3 28.3 %copy-start.6 = (s32[1,3]{1,0:T(1,128)S(1)}, s32[1,3]{1,0:T(1,128)}, u32[]{:S(2)}) copy-start(s32[1,3]{1,0:T(1,128)} %param.21) | copy-start | bytes 40
  36.1 129.7 %all-gather.4.cloned.1.call-start = ((), (), s32[]{:S(2)}) async-start(), calls=%async_computation.1 | async-start | bytes 6758400 | tf_op jit(solution)/shard_map/all_gather | solution.py:70
  36.8 190.9 %all-gather.8.cloned.1.call-start = ((), (), s32[]{:S(2)}) async-start(), calls=%async_computation.4 | async-start | bytes 6488064 | tf_op jit(solution)/shard_map/all_gather | solution.py:37
  38.6 277.4 %all-reduce.2.cloned.1.call-start = ((), (), s32[]{:S(2)}) async-start(), calls=%async_computation.2 | async-start | bytes 5242880 | tf_op jit(solution)/shard_map/psum | solution.py:73
  227.7 88.3 %copy-start.1 = (bf16[1,32,5120]{2,1,0:T(8,128)(2,1)S(1)}, bf16[1,32,5120]{2,1,0:T(8,128)(2,1)}, u32[]{:S(2)}) copy-start(bf16[1,32,5120]{2,1,0:T(8,128)(2,1)} %param.17) | copy-start | bytes 983044
  237.6 81.5 %copy-start.4 = (bf16[5120]{0:T(1024)(128)(2,1)S(1)}, bf16[5120]{0:T(1024)(128)(2,1)}, u32[]{:S(2)}) copy-start(bf16[5120]{0:T(1024)(128)(2,1)} %param.20) | copy-start | bytes 30724
Sparse Core Ops, SparseCore 0:
  36.2 74.6 all-gather.5
  113.4 52.2 all-gather.3
  168.8 58.8 all-gather.7
  229.9 86.0 all-reduce.1
where the time goes:
time: 345 us; the launch traced here: 344 us
  waiting for transfers between devices  237 us (69%)
  blocking collectives  38.1 us (11%)
  other arithmetic  20.9 us (6%)
  matrix products  19.1 us (6%)
  between operations  15.8 us (5%)
  local copies, waits for them, and re-layouts  13.1 us (4%)
    psum x1, waiting for transfers between devices, body(): lax.psum(term_rows.astype(jnp.bfloat16), 'tensor').astype(jnp.float32)  72.1 us
    all_gather x1, waiting for transfers between devices, encode(): whole_rows = lax.all_gather(rows_in, 'tensor', axis=3, tiled=True)  66.2 us
    all_gather x1, waiting for transfers between devices, body(): lax.all_gather(out_weight, 'dp', axis=1, tiled=True)  50.6 us
    all_gather x1, waiting for transfers between devices, encode(): portion = lax.all_gather(blend_weight, 'dp', axis=0, tiled=True)  47.1 us
    all_to_all x1, blocking collectives, body(): lax.all_to_all(outgoing, 'dp', split_axis=0, concat_axis=0, tiled=True)  21 us
    psum x1, blocking collectives, body(): cand_score = lax.psum(vote_sums, 'tensor')  17.1 us
    dot_general x1, matrix products, encode(): jnp.dot(blend_normed, portion.reshape(portion.shape[0], columns), preferr...  9.89 us
    convert_element_type x1, other arithmetic, encode(): (as_float * scale_rows * blend_gain.astype(jnp.float32)).astype(jnp.bfloa...  8.16 us
  transfers between devices with their start and end apart: 4, of which 4 were waited for; matrix products, arithmetic and copies ran while one was open for 12% of the time, Pallas kernels for 0%

commit v1 on v0

--- a/solution.py
+++ b/solution.py
@@ -6,6 +6,19 @@
 
 HR = 40
 HDR = 128
+
+
+def collect(value, axis, dim):
+    ways = lax.axis_size(axis)
+    up = [(d, (d + 1) % ways) for d in range(ways)]
+    down = [(d, (d - 1) % ways) for d in range(ways)]
+    earlier, later = ([value], [value])
+    for _ in range(ways // 2):
+        earlier.append(lax.ppermute(earlier[-1], axis, up))
+    for _ in range((ways - 1) // 2):
+        later.append(lax.ppermute(later[-1], axis, down))
+    line = jnp.concatenate([*earlier[::-1], *later[1:]], axis=dim)
+    return jnp.roll(line, (lax.axis_index(axis) - ways // 2) * value.shape[dim], axis=dim)
 
 
 def pair_attention(queries, keys_in, values_in, head_count):
@@ -27,7 +40,7 @@
 
 
 def encode(rows_in, blend_gain, blend_weight):
-    whole_rows = lax.all_gather(rows_in, "tensor", axis=3, tiled=True)
+    whole_rows = collect(rows_in, "tensor", 3)
     prompts, pick_count, length, features = whole_rows.shape
     flat_rows = whole_rows.reshape(prompts * pick_count * length, features)
     as_float = flat_rows.astype(jnp.float32)

time: 345 us -> 266 us (0.77)
  waiting for transfers between devices: 237 us -> 124 us
  local copies, waits for them, and re-layouts: 13.1 us -> 32.4 us
  starting transfers between devices: 0.16 us -> 12.1 us
    all_gather x1 -> x0, waiting for transfers between devices: 66.2 us -> none  [encode(): whole_rows = lax.all_gather(rows_in, 'tensor', axis=3, tiled=True)]
    ppermute x0 -> x7, waiting for transfers between devices: none -> 61.5 us  [the longest x4 58.4 us: collect(): earlier.append(lax.ppermute(earlier[-1], axis, up))]
    all_gather x1, waiting for transfers between devices: 50.6 us -> 0.02 us  [body(): lax.all_gather(out_weight, 'dp', axis=1, tiled=True)]
    all_gather x1, waiting for transfers between devices: 47.1 us -> 0.01 us  [encode(): portion = lax.all_gather(blend_weight, 'dp', axis=0, tiled=True)]
    unnamed x16 -> x33, local copies, waits for them, and re-layouts: 4.41 us -> 22 us
    ppermute x0 -> x7, starting transfers between devices: none -> 12 us  [the longest x3 9.95 us: collect(): later.append(lax.ppermute(later[-1], axis, down))]
    psum x1, waiting for transfers between devices: 72.1 us -> 62.2 us  [body(): lax.psum(term_rows.astype(jnp.bfloat16), 'tensor').astype(jnp.float32)]
  transfers between devices with their start and end apart: 4 -> 10, of which waited for: 4 -> 6; matrix products, arithmetic and copies ran while one was open for 12% -> 24% of each run, Pallas kernels for 0% -> 0%
where the time goes in v1:
time: 266 us; the launch traced here: 265 us
  waiting for transfers between devices  124 us (47%)
  blocking collectives  40.2 us (15%)
  local copies, waits for them, and re-layouts  32.4 us (12%)
  matrix products  22.2 us (8%)
  other arithmetic  18 us (7%)
  between operations  15.9 us (6%)
  starting transfers between devices  12.1 us (5%)
    psum x1, waiting for transfers between devices, body(): lax.psum(term_rows.astype(jnp.bfloat16), 'tensor').astype(jnp.float32)  62.2 us
    ppermute x4, waiting for transfers between devices, collect(): earlier.append(lax.ppermute(earlier[-1], axis, up))  58.4 us
    all_to_all x1, blocking collectives, body(): lax.all_to_all(outgoing, 'dp', split_axis=0, concat_axis=0, tiled=True)  23.2 us
    unnamed x33, local copies, waits for them, and re-layouts  22 us
    psum x1, blocking collectives, body(): cand_score = lax.psum(vote_sums, 'tensor')  17.1 us
    dot_general x1, matrix products, encode(): jnp.dot(blend_normed, portion.reshape(portion.shape[0], columns), preferr...  10.1 us
    ppermute x3, starting transfers between devices, collect(): later.append(lax.ppermute(later[-1], axis, down))  9.95 us
    convert_element_type x1, other arithmetic, encode(): (as_float * scale_rows * blend_gain.astype(jnp.float32)).astype(jnp.bfloa...  8.13 us
  transfers between devices with their start and end apart: 10, of which 6 were waited for; matrix products, arithmetic and copies ran while one was open for 24% of the time, Pallas kernels for 0%

profile of v1, /device:TPU:2, one launch (start us, length us, event | category | flops | bytes accessed | tf_op | source)
XLA Modules:
  0.0 265.3 jit_solution(11634454347797833627)
XLA Ops:
  7.2 0.0 all-gather.3.cloned.1.call-start
  7.2 0.7 all-gather.3.cloned.1.call-update
  7.9 0.0 all-gather.5.cloned.1.call-start
  8.0 1.7 copy.63
  9.7 0.0 all-gather.5.cloned.1.call-update
  9.7 0.0 all-reduce.2.cloned.1.call-start
  9.8 0.7 select_reduce_fusion.2
  10.5 0.1 copy.60
  10.6 0.1 reshape.142
  10.7 0.1 copy.59
  10.8 1.0 gather_fusion
  11.8 0.8 select_reduce_fusion
  12.6 0.1 iota_compare_fusion
  12.7 1.1 broadcast_select_fusion
  13.8 2.6 gather_fusion.1
  16.4 23.2 %all_to_all.5 = bf16[32,3,8,512]{3,2,1,0:T(8,128)(2,1)S(1)} all-to-all(bf16[32,3,8,512]{3,2,1,0:T(8,128)(2,1)} %gather_fusion.1), channel_id=1, replica_groups=mesh['dp'=32,'tensor'=8] {'dp'}, dimensions={0} | all-to-all | bytes 1572864 | tf_op jit(solution)/shard_map/all_to_all | solution.py:121
  39.5 2.0 collective-permute-start
  41.6 22.2 %collective-permute-done = bf16[32,3,8,512]{3,2,1,0:T(8,128)(2,1)S(1)} collective-permute-done((bf16[32,3,8,512]{3,2,1,0:T(8,128)(2,1)S(1)}, bf16[32,3,8,512]{3,2,1,0:T(8,128)(2,1)S(1)}, u32[]{:S(2)}, u32[]{:S(2)}) %collective-permute-start) | collective-permute-done | bytes 786464 | tf_op jit(solution)/shard_map/ppermute | solution.py:17
  63.8 3.2 %collective-permute-start.4 = (bf16[32,3,8,512]{3,2,1,0:T(8,128)(2,1)S(1)}, bf16[32,3,8,512]{3,2,1,0:T(8,128)(2,1)}, u32[]{:S(2)}, u32[]{:S(2)}) collective-permute-start(bf16[32,3,8,512]{3,2,1,0:T(8,128)(2,1)S(1)} %all_to_all.5), channel_id=1, source_target_pairs={{0,7},{1,0},{2,1},{3,2},{4,3},{5,4},{6,5},{7,6},{8,15},{9,8},{10,9... | collective-permute-start | bytes 2359304 | tf_op jit(solution)/shard_map/ppermute | solution.py:19
  67.0 16.7 %collective-permute-done.1 = bf16[32,3,8,512]{3,2,1,0:T(8,128)(2,1)S(1)} collective-permute-done((bf16[32,3,8,512]{3,2,1,0:T(8,128)(2,1)S(1)}, bf16[32,3,8,512]{3,2,1,0:T(8,128)(2,1)S(1)}, u32[]{:S(2)}, u32[]{:S(2)}) %collective-permute-start.1) | collective-permute-done | bytes 786464 | tf_op jit(solution)/shard_map/ppermute | solution.py:17
  83.7 3.2 %collective-permute-start.5 = (bf16[32,3,8,512]{3,2,1,0:T(8,128)(2,1)}, bf16[32,3,8,512]{3,2,1,0:T(8,128)(2,1)}, u32[]{:S(2)}, u32[]{:S(2)}) collective-permute-start(bf16[32,3,8,512]{3,2,1,0:T(8,128)(2,1)} %collective-permute-done.4), channel_id=1, source_target_pairs={{0,7},{1,0},{2,1},{3,2},{4,3},{5,4},{6,5},{7,6},{8,15},{9,8},{10,9... | collective-permute-start | bytes 2359304 | tf_op jit(solution)/shard_map/ppermute | solution.py:19
  86.9 15.9 %collective-permute-done.2 = bf16[32,3,8,512]{3,2,1,0:T(8,128)(2,1)} collective-permute-done((bf16[32,3,8,512]{3,2,1,0:T(8,128)(2,1)S(1)}, bf16[32,3,8,512]{3,2,1,0:T(8,128)(2,1)}, u32[]{:S(2)}, u32[]{:S(2)}) %collective-permute-start.2) | collective-permute-done | bytes 786464 | tf_op jit(solution)/shard_map/ppermute | solution.py:17
  102.8 0.7 convert_element_type.58
  103.5 2.0 fusion.32
  105.5 1.4 convolution_multiply_fusion
  106.9 2.1 fusion.6
  109.0 1.1 copy.58
  110.1 0.7 convert_element_type.54
  110.8 1.3 fusion.31
  114.1 3.5 %collective-permute-start.6 = (bf16[32,3,8,512]{3,2,1,0:T(8,128)(2,1)}, bf16[32,3,8,512]{3,2,1,0:T(8,128)(2,1)S(1)}, u32[]{:S(2)}, u32[]{:S(2)}) collective-permute-start(bf16[32,3,8,512]{3,2,1,0:T(8,128)(2,1)} %collective-permute-done.5), channel_id=1, source_target_pairs={{0,7},{1,0},{2,1},{3,2},{4,3},{5,4},{6,5},{7,6},{8,15},{9,8},{10,9... | collective-permute-start | bytes 2359304 | tf_op jit(solution)/shard_map/ppermute | solution.py:19
  117.6 3.6 %collective-permute-done.3 = bf16[32,3,8,512]{3,2,1,0:T(8,128)(2,1)} collective-permute-done((bf16[32,3,8,512]{3,2,1,0:T(8,128)(2,1)}, bf16[32,3,8,512]{3,2,1,0:T(8,128)(2,1)}, u32[]{:S(2)}, u32[]{:S(2)}) %collective-permute-start.3) | collective-permute-done | bytes 786464 | tf_op jit(solution)/shard_map/ppermute | solution.py:17
  121.2 1.2 constant_dynamic-update-slice_fusion.15
  122.4 1.2 constant_dynamic-update-slice_fusion.14
  123.7 1.2 constant_dynamic-update-slice_fusion.13
  124.9 1.4 constant_dynamic-update-slice_fusion.12
  126.3 0.1 constant_dynamic-update-slice_fusion.11
  126.4 1.3 constant_dynamic-update-slice_fusion.10
  127.6 1.2 constant_dynamic-update-slice_fusion.9
  128.9 3.2 %collective-permute-done.6 = bf16[32,3,8,512]{3,2,1,0:T(8,128)(2,1)S(1)} collective-permute-done((bf16[32,3,8,512]{3,2,1,0:T(8,128)(2,1)}, bf16[32,3,8,512]{3,2,1,0:T(8,128)(2,1)S(1)}, u32[]{:S(2)}, u32[]{:S(2)}) %collective-permute-start.6) | collective-permute-done | bytes 786464 | tf_op jit(solution)/shard_map/ppermute | solution.py:19
  132.0 0.1 constant_dynamic-update-slice_fusion.8
  132.1 1.4 constant_dynamic-update-slice_fusion.7
  133.5 1.2 constant_dynamic-update-slice_fusion.6
  134.7 0.1 constant_dynamic-update-slice_fusion.5
  134.9 0.1 constant_dynamic-update-slice_fusion.4
  135.0 0.1 constant_dynamic-update-slice_fusion.3
  135.1 1.2 constant_dynamic-update-slice_fusion.2
  136.3 1.2 constant_dynamic-update-slice_fusion.1
  137.5 0.1 constant_dynamic-update-slice_fusion
  137.7 4.6 %copy-done.1 = bf16[32,3,8,8192]{3,2,1,0:T(8,128)(2,1)} copy-done((bf16[32,3,8,8192]{3,2,1,0:T(8,128)(2,1)}, bf16[32,3,8,8192]{3,2,1,0:T(8,128)(2,1)S(1)}, u32[]{:S(2)}) %copy-start.1) | copy-done | bytes 12582936
  142.2 1.3 fusion.1
  143.5 0.1 copy.61
  143.6 0.1 copy.62
  143.7 0.0 all-gather.3.cloned.1.call-done
  143.8 6.6 %convolution_convert_fusion = bf16[256,5120]{1,0:T(8,128)(2,1)} fusion(bf16[640,5120]{0,1:T(8,128)(2,1)} %all-gather.3.cloned.1.call-done, bf16[32,8,5,128]{3,2,1,0:T(8,128)(2,1)S(1)} %bitcast.74), kind=kOutput, calls=%fused_computation.8 | convolution fusion | flops 1679032320 | bytes 9502720 | tf_op jit(solution)/shard_map/dot_general | solution.py:81
  150.4 8.1 %fusion.3 = bf16[32,3,8,4096]{3,2,1,0:T(8,128)(2,1)} fusion(f32[4096]{0:T(1024)S(1)} %convert_element_type.58, f32[32,3,8]{2,1,0:T(4,128)S(1)} %copy.62, bf16[32,3,8,8192]{3,2,1,0:T(8,128)(2,1)} %copy-done.1, s32[]{:T(128)S(6)} %select_n.76), kind=kLoop, calls=%fused_computation.7 | loop fusion | flops 12582912 | bytes 12602372 | tf_op jit(solution)/shard_map/convert_element_type | solution.py:48
  158.6 10.1 %convolution_convert_fusion.1 = bf16[768,768]{1,0:T(8,128)(2,1)} fusion(bf16[768,4096]{1,0:T(8,128)(2,1)} %bitcast.72, bf16[4096,768]{0,1:T(8,128)(2,1)} %bitcast.76), kind=kOutput, calls=%fused_computation.9 | convolution fusion | flops 4832428032 | bytes 13762560 | tf_op jit(solution)/shard_map/dot_general | solution.py:51
  168.7 3.7 %reshape.140 = bf16[32,24,3,256]{3,2,1,0:T(4,128)(2,1)} reshape(bf16[768,768]{1,0:T(8,128)(2,1)} %convolution_convert_fusion.1) | data formatting | bytes 2359296 | tf_op jit(solution)/shard_map/reshape | solution.py:54
  172.4 2.6 copy.64
  175.0 62.2 %all-reduce.2.cloned.1.call-done = bf16[256,5120]{1,0:T(8,128)(2,1)} async-done(((bf16[256,5120]{1,0:T(8,128)(2,1)}), bf16[256,5120]{1,0:T(8,128)(2,1)}) %all-reduce.2.cloned.1.call-update) | async-done | bytes 2621456 | tf_op jit(solution)/shard_map/psum | solution.py:86
  237.2 1.2 multiply_reduce_fusion
  238.4 1.8 fusion.7
  240.3 0.7 multiply_reduce_fusion.1
  241.0 0.7 select_subtract_fusion
  241.7 17.1 %psum.15 = f32[32,8]{0,1:T(8,128)} all-reduce(f32[32,8]{0,1:T(8,128)S(1)} %select_subtract_fusion), channel_id=1, replica_groups=mesh['dp'=32,'tensor'=8] {'tensor'}, use_global_device_ids=true, to_apply=%region_5.6 | all-reduce | flops 256 | bytes 2048 | tf_op jit(solution)/shard_map/psum | solution.py:105
  (28 shorter events, 0.1 us)
Async XLA Ops:
  7.2 3.6 %copy-start = (bf16[32,8,8,512]{3,2,1,0:T(8,128)(2,1)S(1)}, bf16[32,8,8,512]{3,2,1,0:T(8,128)(2,1)}, u32[]{:S(2)}) copy-start(bf16[32,8,8,512]{3,2,1,0:T(8,128)(2,1)} %param.25) | copy-start | bytes 6291460
  7.2 136.6 %all-gather.3.cloned.1.call-start = ((), (), s32[]{:S(2)}) async-start(), calls=%async_computation.1 | async-start | bytes 6758400 | tf_op jit(solution)/shard_map/all_gather | solution.py:83
  7.9 150.7 %all-gather.5.cloned.1.call-start = ((), (), s32[]{:S(2)}) async-start(), calls=%async_computation.3 | async-start | bytes 6488064 | tf_op jit(solution)/shard_map/all_gather | solution.py:50
  9.7 227.5 %all-reduce.2.cloned.1.call-start = ((), (), s32[]{:S(2)}) async-start(), calls=%async_computation.2 | async-start | bytes 5242880 | tf_op jit(solution)/shard_map/psum | solution.py:86
  39.5 24.2 %collective-permute-start = (bf16[32,3,8,512]{3,2,1,0:T(8,128)(2,1)S(1)}, bf16[32,3,8,512]{3,2,1,0:T(8,128)(2,1)S(1)}, u32[]{:S(2)}, u32[]{:S(2)}) collective-permute-start(bf16[32,3,8,512]{3,2,1,0:T(8,128)(2,1)S(1)} %all_to_all.5), channel_id=1, source_target_pairs={{0,1},{1,2},{2,3},{3,4},{4,5},{5,6},{6,7},{7,0},{8,9},{9,10},{10,1... | collective-permute-start | bytes 2359304 | tf_op jit(solution)/shard_map/ppermute | solution.py:17
  63.8 19.9 %copy-start.2 = (bf16[32,3,8,512]{3,2,1,0:T(8,128)(2,1)}, bf16[32,3,8,512]{3,2,1,0:T(8,128)(2,1)S(1)}, u32[]{:S(2)}) copy-start(bf16[32,3,8,512]{3,2,1,0:T(8,128)(2,1)S(1)} %collective-permute-done) | copy-start | bytes 2359300
  63.8 19.9 %collective-permute-start.1 = (bf16[32,3,8,512]{3,2,1,0:T(8,128)(2,1)S(1)}, bf16[32,3,8,512]{3,2,1,0:T(8,128)(2,1)S(1)}, u32[]{:S(2)}, u32[]{:S(2)}) collective-permute-start(bf16[32,3,8,512]{3,2,1,0:T(8,128)(2,1)S(1)} %collective-permute-done), channel_id=1, source_target_pairs={{0,1},{1,2},{2,3},{3,4},{4,5},{5,6},{6,7},{7,0},{8,9},{9,10},{10,1... | collective-permute-start | bytes 2359304 | tf_op jit(solution)/shard_map/ppermute | solution.py:17
  63.8 19.9 %collective-permute-start.4 = (bf16[32,3,8,512]{3,2,1,0:T(8,128)(2,1)S(1)}, bf16[32,3,8,512]{3,2,1,0:T(8,128)(2,1)}, u32[]{:S(2)}, u32[]{:S(2)}) collective-permute-start(bf16[32,3,8,512]{3,2,1,0:T(8,128)(2,1)S(1)} %all_to_all.5), channel_id=1, source_target_pairs={{0,7},{1,0},{2,1},{3,2},{4,3},{5,4},{6,5},{7,6},{8,15},{9,8},{10,9... | collective-permute-start | bytes 2359304 | tf_op jit(solution)/shard_map/ppermute | solution.py:19
  83.7 3.2 %copy-start.4 = (bf16[32,3,8,512]{3,2,1,0:T(8,128)(2,1)}, bf16[32,3,8,512]{3,2,1,0:T(8,128)(2,1)S(1)}, u32[]{:S(2)}) copy-start(bf16[32,3,8,512]{3,2,1,0:T(8,128)(2,1)S(1)} %collective-permute-done.1) | copy-start | bytes 2359300
  83.7 19.1 %collective-permute-start.2 = (bf16[32,3,8,512]{3,2,1,0:T(8,128)(2,1)S(1)}, bf16[32,3,8,512]{3,2,1,0:T(8,128)(2,1)}, u32[]{:S(2)}, u32[]{:S(2)}) collective-permute-start(bf16[32,3,8,512]{3,2,1,0:T(8,128)(2,1)S(1)} %collective-permute-done.1), channel_id=1, source_target_pairs={{0,1},{1,2},{2,3},{3,4},{4,5},{5,6},{6,7},{7,0},{8,9},{9,10},{10,1... | collective-permute-start | bytes 2359304 | tf_op jit(solution)/shard_map/ppermute | solution.py:17
  83.7 30.4 %collective-permute-start.5 = (bf16[32,3,8,512]{3,2,1,0:T(8,128)(2,1)}, bf16[32,3,8,512]{3,2,1,0:T(8,128)(2,1)}, u32[]{:S(2)}, u32[]{:S(2)}) collective-permute-start(bf16[32,3,8,512]{3,2,1,0:T(8,128)(2,1)} %collective-permute-done.4), channel_id=1, source_target_pairs={{0,7},{1,0},{2,1},{3,2},{4,3},{5,4},{6,5},{7,6},{8,15},{9,8},{10,9... | collective-permute-start | bytes 2359304 | tf_op jit(solution)/shard_map/ppermute | solution.py:19
  102.8 18.4 %collective-permute-start.3 = (bf16[32,3,8,512]{3,2,1,0:T(8,128)(2,1)}, bf16[32,3,8,512]{3,2,1,0:T(8,128)(2,1)}, u32[]{:S(2)}, u32[]{:S(2)}) collective-permute-start(bf16[32,3,8,512]{3,2,1,0:T(8,128)(2,1)} %collective-permute-done.2), channel_id=1, source_target_pairs={{0,1},{1,2},{2,3},{3,4},{4,5},{5,6},{6,7},{7,0},{8,9},{9,10},{10,1... | collective-permute-start | bytes 2359304 | tf_op jit(solution)/shard_map/ppermute | solution.py:17
  114.1 20.7 %copy-start.5 = (bf16[32,3,8,512]{3,2,1,0:T(8,128)(2,1)S(1)}, bf16[32,3,8,512]{3,2,1,0:T(8,128)(2,1)}, u32[]{:S(2)}) copy-start(bf16[32,3,8,512]{3,2,1,0:T(8,128)(2,1)} %copy-done.4) | copy-start | bytes 2359300
  114.1 20.8 %copy-start.3 = (bf16[32,3,8,512]{3,2,1,0:T(8,128)(2,1)S(1)}, bf16[32,3,8,512]{3,2,1,0:T(8,128)(2,1)}, u32[]{:S(2)}) copy-start(bf16[32,3,8,512]{3,2,1,0:T(8,128)(2,1)} %copy-done.2) | copy-start | bytes 2359300
  114.1 17.9 %collective-permute-start.6 = (bf16[32,3,8,512]{3,2,1,0:T(8,128)(2,1)}, bf16[32,3,8,512]{3,2,1,0:T(8,128)(2,1)S(1)}, u32[]{:S(2)}, u32[]{:S(2)}) collective-permute-start(bf16[32,3,8,512]{3,2,1,0:T(8,128)(2,1)} %collective-permute-done.5), channel_id=1, source_target_pairs={{0,7},{1,0},{2,1},{3,2},{4,3},{5,4},{6,5},{7,6},{8,15},{9,8},{10,9... | collective-permute-start | bytes 2359304 | tf_op jit(solution)/shard_map/ppermute | solution.py:19
  137.7 4.6 %copy-start.1 = (bf16[32,3,8,8192]{3,2,1,0:T(8,128)(2,1)}, bf16[32,3,8,8192]{3,2,1,0:T(8,128)(2,1)S(1)}, u32[]{:S(2)}) copy-start(bf16[32,3,8,8192]{3,2,1,0:T(8,128)(2,1)S(1)} %constant_dynamic-update-slice_fusion) | copy-start | bytes 37748740
  158.6 78.6 %copy-start.6 = (bf16[1,32,5120]{2,1,0:T(8,128)(2,1)S(1)}, bf16[1,32,5120]{2,1,0:T(8,128)(2,1)}, u32[]{:S(2)}) copy-start(bf16[1,32,5120]{2,1,0:T(8,128)(2,1)} %param.17) | copy-start | bytes 983044
  158.6 81.7 %copy-start.7 = (bf16[5120]{0:T(1024)(128)(2,1)S(1)}, bf16[5120]{0:T(1024)(128)(2,1)}, u32[]{:S(2)}) copy-start(bf16[5120]{0:T(1024)(128)(2,1)} %param.20) | copy-start | bytes 30724
Sparse Core Ops, SparseCore 0:
  10.6 61.8 all-gather.2
  74.9 58.8 all-gather.4
  150.6 86.6 all-reduce.1
